TPU v7x, 512 devices: a whole 4x4x16 slice. The times are simulated.
512 devices in a mesh: freq: 64 (over y, z), space: 8 (over x, core).
Axes of the slice: x: 4, y: 4, z: 16, core: 2. Of those that a mesh axis runs over, the one named last changes fastest.
Arguments:
- snapshots: bfloat16 [64, 256, 3, 2048], P('freq', None, None, 'space'), may hold values from -6 to 6
- point_weights: float32 [2048], P('space'), may hold values from 0.25 to 2
- owner_map: int32 [128], replicated, may hold values from 0 to 127, as said below
- triad_list: int32 [512, 2], replicated, may hold values from 0 to 127, as said below
Outputs:
- power_map: float32 [128, 2048], P('freq', 'space')
- coefficients: float32 [512, 2, 64], P('freq')
- modes: float32 [512, 2, 3, 2048], P('freq', None, None, 'space')
Inputs may be any that keep to these rules, and one draw needn't show every extreme that they name: `owner_map`: A permutation of the 128 frequencies. triad_list[t, 0] + triad_list[t, 1] = owner_map[(t // 8) * 2 + t % 2], and triad_list[t, 0] = 0 when t % 8 == 0 or when that sum is 127.
All inputs are finite; a program needn't handle non-finite values.
Results may differ from a plain program's by a relative error of at most 0.005.
The roundings to bfloat16 on the way count: a program that leaves them out, or rounds other values in their place, can miss the bound.
Values may be sent and summed in bfloat16 or wider, within the bound.
A program may use at most 64 MiB of HBM per device.

v0:
```python
import math

import jax
import jax.numpy as jnp
from jax import lax
from jax.sharding import PartitionSpec as P


def make_table(samples, frequencies):
    sample_idx = jnp.arange(samples, dtype=jnp.int32)
    freq_idx = jnp.arange(frequencies, dtype=jnp.int32)
    angles = (freq_idx[:, None] * sample_idx[None, :] % samples).astype(jnp.float32) * (
        2.0 * math.pi / samples
    )
    window = 0.5 - 0.5 * jnp.cos(sample_idx.astype(jnp.float32) * (2.0 * math.pi / samples))
    taper = window / math.sqrt(samples)
    stacked = jnp.stack([jnp.cos(angles) * taper, -jnp.sin(angles) * taper], axis=1)
    return stacked.reshape(2 * frequencies, samples).astype(jnp.bfloat16)


def normalized(vec_real, vec_imag):
    energy = jnp.mean(vec_real * vec_real + vec_imag * vec_imag, axis=-1, keepdims=True)
    factor = lax.rsqrt(energy + 1e-05)
    return (vec_real * factor, vec_imag * factor)


def leading_vector(gram_real, gram_imag):
    vec_real = jnp.ones(gram_real.shape[:-1], jnp.float32)
    vec_imag = jnp.zeros(gram_real.shape[:-1], jnp.float32)
    for sweep in range(2):
        next_real = jnp.einsum(
            "tij,tj->ti", gram_real, vec_real, precision=lax.Precision.HIGHEST
        ) - jnp.einsum("tij,tj->ti", gram_imag, vec_imag, precision=lax.Precision.HIGHEST)
        next_imag = jnp.einsum(
            "tij,tj->ti", gram_real, vec_imag, precision=lax.Precision.HIGHEST
        ) + jnp.einsum("tij,tj->ti", gram_imag, vec_real, precision=lax.Precision.HIGHEST)
        vec_real, vec_imag = normalized(next_real, next_imag)
    return (vec_real, vec_imag)


def body(snapshots, point_weights, owner_map, triad_list):
    samples = snapshots.shape[1]
    points = snapshots.shape[3]
    columns = 3 * points
    frequencies = owner_map.shape[0]
    triad_count = triad_list.shape[0]
    block_count = lax.axis_size("freq")
    triads_here = triad_count // block_count
    dft_table = make_table(samples, frequencies)
    spectra = jnp.dot(
        dft_table, snapshots.reshape(samples, columns), preferred_element_type=jnp.float32
    )
    spectra = spectra.astype(jnp.bfloat16).reshape(frequencies, 2, columns)
    first_freq = triad_list[:, 0]
    second_freq = triad_list[:, 1]
    first_rows = jnp.take(spectra, first_freq, axis=0).astype(jnp.float32)
    second_rows = jnp.take(spectra, second_freq, axis=0).astype(jnp.float32)
    point_weight = jnp.tile(point_weights, 3)
    prod_real = (
        first_rows[:, 0] * second_rows[:, 0] - first_rows[:, 1] * second_rows[:, 1]
    ) * point_weight
    prod_imag = (
        first_rows[:, 0] * second_rows[:, 1] + first_rows[:, 1] * second_rows[:, 0]
    ) * point_weight
    products = jnp.stack([prod_real, prod_imag], axis=1).astype(jnp.bfloat16)
    spectra_f = spectra.astype(jnp.float32)
    energy = jnp.sum(spectra_f * spectra_f, axis=1).reshape(frequencies, 3, points)
    energy = jnp.sum(energy, axis=1) / block_count
    power_map = lax.psum_scatter(
        jnp.take(energy, owner_map, axis=0), "freq", scatter_dimension=0, tiled=True
    )
    sum_send = jnp.take(spectra, first_freq + second_freq, axis=0)
    received, sum_rows = (
        lax.all_to_all(products[None], "freq", split_axis=1, concat_axis=0, tiled=True),
        lax.all_to_all(sum_send[None], "freq", split_axis=1, concat_axis=0, tiled=True),
    )
    gram_real = jnp.einsum("itrc,jtrc->tij", received, sum_rows, preferred_element_type=jnp.float32)
    gram_imag = jnp.einsum(
        "itc,jtc->tij", received[:, :, 0], sum_rows[:, :, 1], preferred_element_type=jnp.float32
    ) - jnp.einsum(
        "itc,jtc->tij", received[:, :, 1], sum_rows[:, :, 0], preferred_element_type=jnp.float32
    )
    gram_real, gram_imag = lax.psum((gram_real, gram_imag), "space")
    vec_real, vec_imag = leading_vector(gram_real, gram_imag)
    coefficients = jnp.stack([vec_real, vec_imag], axis=1)
    coef_rounded = coefficients.astype(jnp.bfloat16)
    mode_real = jnp.einsum(
        "tb,btc->tc", coef_rounded[:, 0], sum_rows[:, :, 0], preferred_element_type=jnp.float32
    ) - jnp.einsum(
        "tb,btc->tc", coef_rounded[:, 1], sum_rows[:, :, 1], preferred_element_type=jnp.float32
    )
    mode_imag = jnp.einsum(
        "tb,btc->tc", coef_rounded[:, 0], sum_rows[:, :, 1], preferred_element_type=jnp.float32
    ) + jnp.einsum(
        "tb,btc->tc", coef_rounded[:, 1], sum_rows[:, :, 0], preferred_element_type=jnp.float32
    )
    modes = jnp.stack([mode_real, mode_imag], axis=1) / math.sqrt(block_count)
    return (power_map, coefficients, modes.reshape(triads_here, 2, 3, points))


def solution(mesh):
    placed = (P("freq", None, None, "space"), P("space"), P(), P())
    return jax.shard_map(
        body,
        mesh=mesh,
        in_specs=placed,
        out_specs=(P("freq", "space"), P("freq", None, None), P("freq", None, None, "space")),
        check_vma=False,
    )
```

profile of v0, /device:TPU:1, one launch (start us, length us, event | category | flops | bytes accessed | tf_op | source)
XLA Modules:
  0.0 508.2 jit_solution(8572768189631044325)
XLA Ops:
  7.2 0.8 fusion.29
  8.0 0.5 compare_and_fusion
  8.5 0.6 multiply_convert_fusion.3
  9.3 1.2 copy.79
  10.5 0.3 convolution_convert_fusion
  11.0 4.6 gather_fusion.1
  15.5 4.6 gather_fusion.2
  20.1 5.3 %fusion = (f32[512,2,768]{2,1,0:T(2,128)S(1)}, f32[512,2,768]{2,1,0:T(2,128)S(1)}) fusion(bf16[512,2,768]{2,1,0:T(2,128)(2,1)S(1)} %gather_fusion.1, pred[512]{0:T(512)(128)(4,1)S(1)} %get-tuple-element.42, bf16[512,2,768]{2,1,0:T(2,128)(2,1)S(1)} %gather_fusion.2, pred[512]{0:T(512)(128)(4,1)} %get-tuple-element.43), kind=kLoop, calls=%fused_computation.7 | loop fusion | flops 3145728 | bytes 9438208 | tf_op jit(solution)/shard_map/convert_element_type | solution.py:56
  25.5 5.8 %multiply_convert_fusion.1 = (bf16[512,1,768]{2,1,0:T(2,128)(2,1)S(1)}, bf16[512,1,768]{2,1,0:T(2,128)(2,1)S(1)}) fusion(f32[512,2,768]{2,1,0:T(2,128)S(1)} %get-tuple-element.51, f32[512,2,768]{2,1,0:T(2,128)S(1)} %get-tuple-element.50, f32[768]{0:T(1024)S(1)} %mul.191), kind=kLoop, calls=%fused_computation.16 | loop fusion | flops 3932160 | bytes 7867392 | tf_op jit(solution)/shard_map/convert.3
  31.6 2.8 copy.82
  34.4 19.5 %all-to-all-start = ((bf16[1,512,2,768]{3,2,0,1:T(2,128)(2,1)}), bf16[1,512,2,768]{3,2,0,1:T(2,128)(2,1)S(1)}, u32[]{:S(2)}, u32[]{:S(2)}) async-start(bf16[1,512,2,768]{3,2,0,1:T(2,128)(2,1)} %copy.82), calls=%async_computation | async-start | bytes 3145728 | tf_op jit(solution)/shard_map/all_to_all | solution.py:74
  53.9 4.6 gather_fusion.3
  58.5 3.3 fusion.5
  61.7 62.6 %all-to-all-done = bf16[1,512,2,768]{3,2,0,1:T(2,128)(2,1)S(1)} async-done(((bf16[1,512,2,768]{3,2,0,1:T(2,128)(2,1)}), bf16[1,512,2,768]{3,2,0,1:T(2,128)(2,1)S(1)}, u32[]{:S(2)}, u32[]{:S(2)}) %all-to-all-start) | async-done | bytes 1572896 | tf_op jit(solution)/shard_map/all_to_all | solution.py:74
  124.3 12.5 %all-to-all-start.1 = ((bf16[1,512,2,768]{3,2,0,1:T(2,128)(2,1)}), bf16[1,512,2,768]{3,2,0,1:T(2,128)(2,1)S(1)}, u32[]{:S(2)}, u32[]{:S(2)}) async-start(bf16[1,512,2,768]{3,2,0,1:T(2,128)(2,1)} %fusion.5), calls=%async_computation.1 | async-start | bytes 3145728 | tf_op jit(solution)/shard_map/all_to_all | solution.py:75
  136.9 1.8 multiply_reduce_fusion
  138.7 1.1 copy.80
  139.8 0.7 reduce_sum.37
  140.5 1.0 copy.81
  141.5 0.8 gather_fusion
  142.3 0.7 broadcast_select_fusion.3
  143.1 0.2 copy.156
  143.3 1.1 copy-done
  144.5 1.2 fusion.28
  145.7 62.4 %all-to-all-done.1 = bf16[1,512,2,768]{3,2,0,1:T(2,128)(2,1)S(1)} async-done(((bf16[1,512,2,768]{3,2,0,1:T(2,128)(2,1)}), bf16[1,512,2,768]{3,2,0,1:T(2,128)(2,1)S(1)}, u32[]{:S(2)}, u32[]{:S(2)}) %all-to-all-start.1) | async-done | bytes 1572896 | tf_op jit(solution)/shard_map/all_to_all | solution.py:75
  208.5 1.3 copy-done.1
  209.7 1.3 fusion.6
  211.0 0.4 fusion.11
  211.4 0.8 copy-done.4
  212.2 1.1 convolution_subtract_fusion
  213.3 1.3 dynamic-slice
  215.2 191.5 %all-reduce.5.cloned.1.call-done = f32[128,256]{1,0:T(8,128)} async-done(((f32[128,256]{1,0:T(8,128)}), f32[128,256]{1,0:T(8,128)}) %all-reduce.5.cloned.1.call-update) | async-done | bytes 131088
  406.7 1.3 constant_dynamic-slice_fusion
  408.0 80.7 %all-reduce.7.cloned.1.call-done = (f32[8,64,64]{2,1,0:T(8,128)}, f32[8,64,64]{2,1,0:T(8,128)}) async-done(((f32[8,64,64]{2,1,0:T(8,128)}, f32[8,64,64]{2,1,0:T(8,128)}), (f32[8,64,64]{2,1,0:T(8,128)}, f32[8,64,64]{2,1,0:T(8,128)})) %all-reduce.7.cloned.1.call-update) | async-done | bytes 262160 | tf_op jit(solution)/shard_map/psum | solution.py:83
  488.7 1.5 fusion.30
  490.2 1.5 fusion.32
  491.7 1.5 fusion.31
  493.2 1.5 fusion.33
  494.9 1.5 fusion.36
  496.3 1.5 fusion.35
  497.8 0.5 fusion.37
  498.3 0.5 fusion.34
  499.1 0.2 fusion.15
  499.3 0.2 fusion.12
  499.6 0.2 fusion.13
  499.8 0.2 fusion.14
  500.1 0.7 copy.93
  500.8 0.6 copy.92
  (56 shorter events, 1.8 us)
Async XLA Ops:
  15.5 4.6 copy-start.7
  34.4 89.9 %all-to-all-start = ((bf16[1,512,2,768]{3,2,0,1:T(2,128)(2,1)}), bf16[1,512,2,768]{3,2,0,1:T(2,128)(2,1)S(1)}, u32[]{:S(2)}, u32[]{:S(2)}) async-start(bf16[1,512,2,768]{3,2,0,1:T(2,128)(2,1)} %copy.82), calls=%async_computation | async-start | bytes 3145728 | tf_op jit(solution)/shard_map/all_to_all | solution.py:74
  53.9 4.6 copy-start.6
  124.3 83.8 %all-to-all-start.1 = ((bf16[1,512,2,768]{3,2,0,1:T(2,128)(2,1)}), bf16[1,512,2,768]{3,2,0,1:T(2,128)(2,1)S(1)}, u32[]{:S(2)}, u32[]{:S(2)}) async-start(bf16[1,512,2,768]{3,2,0,1:T(2,128)(2,1)} %fusion.5), calls=%async_computation.1 | async-start | bytes 3145728 | tf_op jit(solution)/shard_map/all_to_all | solution.py:75
  136.8 4.7 copy-start.8
  136.8 269.8 %all-reduce.5.cloned.1.call-start = ((), (), s32[]{:S(2)}) async-start(), calls=%async_computation.2 | async-start | bytes 262144
  143.1 345.6 %all-reduce.7.cloned.1.call-start = ((), (), s32[]{:S(2)}) async-start(), calls=%async_computation.3 | async-start | bytes 1048576 | tf_op jit(solution)/shard_map/psum | solution.py:83
  143.3 1.1 copy-start
  208.3 1.4 copy-start.1
  209.7 1.3 copy-start.5
  211.0 1.1 copy-start.4
  488.7 9.1 %copy-start.3 = (f32[8,64,64]{2,1,0:T(8,128)S(1)}, f32[8,64,64]{2,1,0:T(8,128)}, u32[]{:S(2)}) copy-start(f32[8,64,64]{2,1,0:T(8,128)} %get-tuple-element.23) | copy-start | bytes 393220
  488.7 9.7 %copy-start.2 = (f32[8,64,64]{2,1,0:T(8,128)S(1)}, f32[8,64,64]{2,1,0:T(8,128)}, u32[]{:S(2)}) copy-start(f32[8,64,64]{2,1,0:T(8,128)} %get-tuple-element.22) | copy-start | bytes 393220
Sparse Core Ops, SparseCore 0:
  143.2 263.4 all-reduce.4
  409.1 79.5 all-reduce.6
where the time goes:
time: 510 us; the launch traced here: 508 us
  waiting for transfers between devices  397 us (78%)
  starting transfers between devices  32.1 us (6%)
  local copies, waits for them, and re-layouts  30.6 us (6%)
  other arithmetic  19.3 us (4%)
  between operations  15.1 us (3%)
  matrix products  13.9 us (3%)
    unnamed x3, waiting for transfers between devices  191 us
    psum x1, waiting for transfers between devices, body(): gram_real, gram_imag = lax.psum((gram_real, gram_imag), 'space')  80.7 us
    all_to_all x1, waiting for transfers between devices, body(): lax.all_to_all(products[None], 'freq', split_axis=1, concat_axis=0, tiled...  62.6 us
    all_to_all x1, waiting for transfers between devices, body(): lax.all_to_all(sum_send[None], 'freq', split_axis=1, concat_axis=0, tiled...  62.4 us
    all_to_all x1, starting transfers between devices, body(): lax.all_to_all(products[None], 'freq', split_axis=1, concat_axis=0, tiled...  19.5 us
    all_to_all x1, starting transfers between devices, body(): lax.all_to_all(sum_send[None], 'freq', split_axis=1, concat_axis=0, tiled...  12.5 us
  transfers between devices with their start and end apart: 4, of which 4 were waited for; matrix products, arithmetic and copies ran while one was open for 4% of the time, Pallas kernels for 0%

commit v1 on v0

v1 whole, which is shorter than its diff:
```python
import math

import jax
import jax.numpy as jnp
from jax import lax
from jax.sharding import PartitionSpec as P


def make_table(samples, frequencies):
    sample_idx = jnp.arange(samples, dtype=jnp.int32)
    freq_idx = jnp.arange(frequencies, dtype=jnp.int32)
    angles = (freq_idx[:, None] * sample_idx[None, :] % samples).astype(jnp.float32) * (
        2.0 * math.pi / samples
    )
    window = 0.5 - 0.5 * jnp.cos(sample_idx.astype(jnp.float32) * (2.0 * math.pi / samples))
    taper = window / math.sqrt(samples)
    stacked = jnp.stack([jnp.cos(angles) * taper, -jnp.sin(angles) * taper], axis=1)
    return stacked.reshape(2 * frequencies, samples).astype(jnp.bfloat16)


def select_rows(index, rows):
    hot = (index[:, None] == jnp.arange(rows.shape[0], dtype=jnp.int32)[None, :]).astype(jnp.bfloat16)
    return jnp.dot(hot, rows, preferred_element_type=jnp.float32)


def sum_over_space(value):
    spread = jnp.broadcast_to(value[None], (lax.axis_size("space"),) + value.shape)
    return jnp.sum(lax.all_to_all(spread, "space", split_axis=0, concat_axis=0, tiled=True), axis=0)


def normalized(vec_real, vec_imag):
    energy = jnp.mean(vec_real * vec_real + vec_imag * vec_imag, axis=-1, keepdims=True)
    factor = lax.rsqrt(energy + 1e-05)
    return (vec_real * factor, vec_imag * factor)


def weighted_sum(vec_real, vec_imag, sums):
    both = jnp.concatenate([vec_real, vec_imag], axis=1)
    out = jnp.einsum(
        "sub,bsk->suk", both, sums, precision=lax.Precision.HIGHEST, preferred_element_type=jnp.float32
    )
    n, k = vec_real.shape[1], sums.shape[2] // 2
    real = out[:, :n, :k] - out[:, n:, k:]
    imag = out[:, :n, k:] + out[:, n:, :k]
    return (real, imag)


def body(snapshots, point_weights, owner_map, triad_list):
    samples = snapshots.shape[1]
    points = snapshots.shape[3]
    columns = 3 * points
    frequencies = owner_map.shape[0]
    triad_count = triad_list.shape[0]
    block_count = lax.axis_size("freq")
    triads_here = triad_count // block_count
    slots = frequencies // block_count
    dft_table = make_table(samples, frequencies)
    spectra = jnp.dot(
        dft_table, snapshots.reshape(samples, columns), preferred_element_type=jnp.float32
    ).astype(jnp.bfloat16)
    spectra = spectra.reshape(frequencies, 2 * columns)
    first = select_rows(triad_list[:, 0], spectra)
    second = select_rows(triad_list[:, 1], spectra)
    k_real, k_imag = first[:, :columns], first[:, columns:]
    l_real, l_imag = second[:, :columns], second[:, columns:]
    point_weight = jnp.tile(point_weights, 3)
    prod_real = ((k_real * l_real - k_imag * l_imag) * point_weight).astype(jnp.bfloat16)
    prod_imag = ((k_real * l_imag + k_imag * l_real) * point_weight).astype(jnp.bfloat16)
    products = jnp.concatenate([prod_real, prod_imag], axis=1)
    owned = select_rows(owner_map, spectra).astype(jnp.bfloat16)
    packet = jnp.concatenate(
        [
            products.reshape(block_count, triads_here, 2 * columns),
            owned.reshape(block_count, slots, 2 * columns),
        ],
        axis=1,
    )
    packet = lax.all_to_all(packet, "freq", split_axis=0, concat_axis=0, tiled=True)
    sums = packet[:, triads_here:]
    prods = packet[:, :triads_here].astype(jnp.float32)
    prods_real, prods_imag = prods[:, :, :columns], prods[:, :, columns:]
    sums_f = sums.astype(jnp.float32)
    power_map = jnp.sum((sums_f * sums_f).reshape(block_count, slots, 6, points), axis=(0, 2)) / block_count

    per_slot = triads_here // slots

    def apply(field_real, field_imag):
        v_real = jnp.sum(prods_real * field_real + prods_imag * field_imag, axis=2)
        v_imag = jnp.sum(prods_real * field_imag - prods_imag * field_real, axis=2)
        v = sum_over_space(jnp.stack([v_real.T, v_imag.T]))
        return normalized(v[0], v[1])

    def by_triad(x):
        return x.transpose(1, 0, 2).reshape(triads_here, columns)

    def by_slot(x):
        return x.reshape(per_slot, slots, block_count).transpose(1, 0, 2)

    total = jnp.sum(sums_f, axis=0)
    total = jnp.tile(total, (per_slot, 1))
    vec_real, vec_imag = apply(total[:, :columns], total[:, columns:])
    field_real, field_imag = weighted_sum(by_slot(vec_real), by_slot(vec_imag), sums_f)
    vec_real, vec_imag = apply(by_triad(field_real), by_triad(field_imag))
    coefficients = jnp.stack([vec_real, vec_imag], axis=1)
    rounded = lax.reduce_precision(coefficients, exponent_bits=8, mantissa_bits=7)
    mode_real, mode_imag = weighted_sum(by_slot(rounded[:, 0]), by_slot(rounded[:, 1]), sums_f)
    modes = jnp.stack([by_triad(mode_real), by_triad(mode_imag)], axis=1) / math.sqrt(block_count)
    return (power_map, coefficients, modes.reshape(triads_here, 2, 3, points))


def solution(mesh):
    placed = (P("freq", None, None, "space"), P("space"), P(), P())
    return jax.shard_map(
        body,
        mesh=mesh,
        in_specs=placed,
        out_specs=(P("freq", "space"), P("freq", None, None), P("freq", None, None, "space")),
        check_vma=False,
    )
```

time: 510 us -> 222 us (0.44)
  waiting for transfers between devices: 397 us -> 7.66 us
  blocking collectives: 0 us -> 159 us
  starting transfers between devices: 32.1 us -> 12.9 us
  between operations: 15.1 us -> 0.86 us
  local copies, waits for them, and re-layouts: 30.6 us -> 19.8 us
  matrix products: 13.9 us -> 4.81 us
    unnamed x3 -> x0, waiting for transfers between devices: 191 us -> none
    all_to_all x0 -> x1, blocking collectives: none -> 159 us  [body(): lax.all_to_all(packet, 'freq', split_axis=0, concat_axis=0, tiled=True)]
    all_to_all x2, waiting for transfers between devices: 125 us -> 7.66 us  [sum_over_space(): lax.all_to_all(spread, 'space', split_axis=0, concat_axis=0, tiled=True)]
    psum x1 -> x0, waiting for transfers between devices: 80.7 us -> none  [body(): gram_real, gram_imag = lax.psum((gram_real, gram_imag), 'space')]
    all_to_all x2, starting transfers between devices: 32 us -> 12.9 us  [sum_over_space(): lax.all_to_all(spread, 'space', split_axis=0, concat_axis=0, tiled=True)]
    gather x4 -> x0, local copies, waits for them, and re-layouts: 14.4 us -> none  [the longest x1 4.55 us: body(): first_rows = jnp.take(spectra, first_freq, axis=0).astype(jnp.float32)]
    dot_general x15 -> x5, matrix products: 13.6 us -> 4.51 us  [the longest x3 3.95 us: select_rows(): return jnp.dot(hot, rows, preferred_element_type=jnp.float32)]
    another operation x5 -> x3, other arithmetic: 6.54 us -> 0.56 us
  transfers between devices with their start and end apart: 4 -> 2, of which waited for: 4 -> 2; matrix products, arithmetic and copies ran while one was open for 4% -> 1% of each run, Pallas kernels for 0% -> 0%
where the time goes in v1:
time: 222 us; the launch traced here: 220 us
  blocking collectives  159 us (72%)
  local copies, waits for them, and re-layouts  19.8 us (9%)
  other arithmetic  15.1 us (7%)
  starting transfers between devices  12.9 us (6%)
  waiting for transfers between devices  7.66 us (3%)
  matrix products  4.81 us (2%)
    all_to_all x1, blocking collectives, body(): lax.all_to_all(packet, 'freq', split_axis=0, concat_axis=0, tiled=True)  159 us
    all_to_all x2, starting transfers between devices, sum_over_space(): lax.all_to_all(spread, 'space', split_axis=0, concat_axis=0, tiled=True)  12.9 us
    unnamed x21, local copies, waits for them, and re-layouts  11.2 us
    all_to_all x2, waiting for transfers between devices, sum_over_space(): lax.all_to_all(spread, 'space', split_axis=0, concat_axis=0, tiled=True)  7.66 us
  transfers between devices with their start and end apart: 2, of which 2 were waited for; matrix products, arithmetic and copies ran while one was open for 1% of the time, Pallas kernels for 0%

profile of v1, /device:TPU:1, one launch (start us, length us, event | category | flops | bytes accessed | tf_op | source)
XLA Modules:
  0.0 220.5 jit_solution(15491634417190585559)
XLA Ops:
  0.7 0.6 multiply_convert_fusion.3
  1.3 0.1 copy.80
  1.5 1.2 copy.81
  2.6 0.3 convolution_convert_fusion.1
  3.0 0.1 reshape.265
  3.1 0.6 fusion.1
  3.8 2.3 %fusion.2 = f32[512,1536]{1,0:T(8,128)} fusion(bf16[128,1536]{1,0:T(8,128)(2,1)S(1)} %reshape.265, s32[512]{0:T(512)S(1)} %bitcast.55), kind=kOutput, calls=%fused_computation.17 | convolution fusion | flops 201392128 | bytes 3540992 | tf_op jit(solution)/shard_map/dot_general | solution.py:23
  6.1 1.1 convolution_convert_fusion
  7.1 1.1 reshape.267
  8.3 2.4 %multiply_convert_fusion.1 = (bf16[512,768]{1,0:T(8,128)(2,1)S(1)}, bf16[512,768]{1,0:T(8,128)(2,1)S(1)}) fusion(f32[512,1536]{1,0:T(8,128)} %fusion.2, f32[512,1536]{1,0:T(8,128)S(1)} %fusion.1, f32[768]{0:T(1024)S(1)} %mul.264), kind=kLoop, calls=%fused_computation.9 | loop fusion | flops 3932160 | bytes 7867392 | tf_op jit(solution)/shard_map/convert_element_type | solution.py:67
  10.8 0.4 pad_maximum_fusion
  11.2 159.3 %all_to_all.15 = bf16[64,10,1536]{2,1,0:T(8,128)(2,1)S(1)} all-to-all(bf16[64,10,1536]{2,1,0:T(8,128)(2,1)S(1)} %pad_maximum_fusion), channel_id=1, replica_groups=mesh['freq'=64,'space'=8] {'freq'}, dimensions={0} | all-to-all | bytes 3932160 | tf_op jit(solution)/shard_map/all_to_all | solution.py:78
  170.5 1.7 copy-done
  172.1 0.3 slice.108
  172.4 0.7 convert_reduce_fusion
  173.2 1.8 slice_convert_fusion
  175.0 1.2 add_reduce_fusion.1
  176.2 0.8 copy.98
  177.0 0.8 copy.99
  177.9 0.6 broadcast_in_dim.4
  178.5 1.6 reshape.268
  180.1 8.9 %all-to-all-start.1 = ((f32[8,1,1024]{2,1,0:T(1,128)}), f32[8,1,1024]{2,1,0:T(1,128)}, u32[]{:S(2)}, u32[]{:S(2)}) async-start(f32[8,1,1024]{2,1,0:T(1,128)} %reshape.268), calls=%async_computation.1 | async-start | bytes 65536 | tf_op jit(solution)/shard_map/all_to_all | solution.py:28
  189.0 0.7 reduce_sum.98
  189.7 0.6 reduce_sum.99
  190.3 3.5 %all-to-all-done.1 = f32[8,1,1024]{2,1,0:T(1,128)} async-done(((f32[8,1,1024]{2,1,0:T(1,128)}), f32[8,1,1024]{2,1,0:T(1,128)}, u32[]{:S(2)}, u32[]{:S(2)}) %all-to-all-start.1) | async-done | bytes 32800 | tf_op jit(solution)/shard_map/all_to_all | solution.py:28
  193.8 0.5 broadcast.224
  194.3 2.1 reduce.4
  196.4 1.5 reshape.269
  197.9 0.9 reduce_sum.103
  198.7 0.1 fusion.33
  199.1 0.3 fusion.5
  199.4 0.6 fusion.19
  200.0 0.6 copy.88
  200.6 1.4 mul.282
  202.0 1.3 copy.89
  203.3 1.4 mul.285
  204.7 2.0 add_reduce_fusion
  206.6 0.8 copy.100
  207.4 0.8 copy.101
  208.3 0.7 reshape.270
  209.0 4.0 %all-to-all-start.2 = ((f32[8,1,1024]{2,1,0:T(1,128)}), f32[8,1,1024]{2,1,0:T(1,128)S(1)}, u32[]{:S(2)}, u32[]{:S(2)}) async-start(f32[8,1,1024]{2,1,0:T(1,128)} %reshape.270), calls=%async_computation.2 | async-start | bytes 65536 | tf_op jit(solution)/shard_map/all_to_all | solution.py:28
  213.0 0.6 broadcast_multiply_fusion
  213.6 4.2 %all-to-all-done.2 = f32[8,1,1024]{2,1,0:T(1,128)S(1)} async-done(((f32[8,1,1024]{2,1,0:T(1,128)}), f32[8,1,1024]{2,1,0:T(1,128)S(1)}, u32[]{:S(2)}, u32[]{:S(2)}) %all-to-all-start.2) | async-done | bytes 32800 | tf_op jit(solution)/shard_map/all_to_all | solution.py:28
  217.7 0.7 reduce.5
  218.5 0.1 add_reduce_fusion.2
  218.8 0.3 fusion.3
  219.2 0.7 copy.97
  219.9 0.6 copy.96
  (39 shorter events, 0.9 us)
Async XLA Ops:
  1.3 1.8 copy-start.2
  3.7 2.3 %copy-start.3 = (f32[256]{0:T(256)S(1)}, f32[256]{0:T(256)}, u32[]{:S(2)}) copy-start(f32[256]{0:T(256)} %param.5) | copy-start | bytes 3076
  3.7 2.3 %copy-start.4 = (s32[128]{0:T(128)S(1)}, s32[128]{0:T(128)}, u32[]{:S(2)}) copy-start(s32[128]{0:T(128)} %param.6) | copy-start | bytes 1540
  170.5 1.7 copy-start
  180.1 13.7 %all-to-all-start.1 = ((f32[8,1,1024]{2,1,0:T(1,128)}), f32[8,1,1024]{2,1,0:T(1,128)}, u32[]{:S(2)}, u32[]{:S(2)}) async-start(f32[8,1,1024]{2,1,0:T(1,128)} %reshape.268), calls=%async_computation.1 | async-start | bytes 65536 | tf_op jit(solution)/shard_map/all_to_all | solution.py:28
  204.7 8.3 %copy-start.1 = (f32[2,256]{1,0:T(2,128)S(1)}, f32[2,256]{1,0:T(2,128)}, u32[]{:S(2)}) copy-start(f32[2,256]{1,0:T(2,128)} %reduce_sum.99) | copy-start | bytes 6148
  209.0 8.7 %all-to-all-start.2 = ((f32[8,1,1024]{2,1,0:T(1,128)}), f32[8,1,1024]{2,1,0:T(1,128)S(1)}, u32[]{:S(2)}, u32[]{:S(2)}) async-start(f32[8,1,1024]{2,1,0:T(1,128)} %reshape.270), calls=%async_computation.2 | async-start | bytes 65536 | tf_op jit(solution)/shard_map/all_to_all | solution.py:28

commit v2 on v1

v2 whole, which is shorter than its diff:
```python
import functools
import math

import jax
import jax.numpy as jnp
from jax import lax
from jax.experimental import pallas as pl
from jax.experimental.pallas import tpu as pltpu
from jax.sharding import PartitionSpec as P


def make_table(samples, frequencies):
    sample_idx = jnp.arange(samples, dtype=jnp.int32)
    freq_idx = jnp.arange(frequencies, dtype=jnp.int32)
    angles = (freq_idx[:, None] * sample_idx[None, :] % samples).astype(jnp.float32) * (
        2.0 * math.pi / samples
    )
    window = 0.5 - 0.5 * jnp.cos(sample_idx.astype(jnp.float32) * (2.0 * math.pi / samples))
    taper = window / math.sqrt(samples)
    stacked = jnp.stack([jnp.cos(angles) * taper, -jnp.sin(angles) * taper], axis=1)
    return stacked.reshape(2 * frequencies, samples).astype(jnp.bfloat16)


def select_rows(index, rows):
    hot = (index[:, None] == jnp.arange(rows.shape[0], dtype=jnp.int32)[None, :]).astype(jnp.bfloat16)
    return jnp.dot(hot, rows, preferred_element_type=jnp.float32)


MESH = pl.DeviceIdType.MESH
LANES = 128


def kernel(
    nq, ne, spec_ref, own_ref, weight_ref, triad_ref,
    coef_ref, sums_ref,
    spec_all, flat, rows, prod_re, prod_im, sum_re, sum_im, field,
    part, part_in, piece, piece_in, mine, gathered, spread,
    send_sem, recv_sem,
):
    q = lax.axis_index("freq")
    e = lax.axis_index("space")
    blocks, cols, width = spec_ref.shape
    pad = flat.shape[1] // blocks
    triads = triad_ref.shape[1]
    per_e = blocks // ne
    groups = triads // LANES

    barrier = pltpu.get_barrier_semaphore()

    def others(axis, count, index, act):
        def step(i, carry):
            act({axis: lax.rem(index + i, count)}, lax.rem(index + i, count))
            return carry

        lax.fori_loop(1, count, step, 0)

    def greet(device, _):
        pl.semaphore_signal(barrier, inc=1, device_id=device, device_id_type=MESH)

    others("freq", nq, q, greet)
    others("space", ne, e, greet)
    pl.semaphore_wait(barrier, nq + ne - 2)

    def exchange(slot, axis, count, index, source, target):
        def act(device, i):
            pltpu.make_async_remote_copy(
                src_ref=source(i), dst_ref=target.at[index],
                send_sem=send_sem.at[slot], recv_sem=recv_sem.at[slot],
                device_id=device, device_id_type=MESH,
            ).start()

        pltpu.make_async_copy(source(index), target.at[index], recv_sem.at[slot]).start()
        others(axis, count, index, act)

        def finish():
            pltpu.make_async_copy(target, target, recv_sem.at[slot]).wait()
            rest = target.at[pl.ds(0, count - 1)]
            pltpu.make_async_copy(rest, rest, send_sem.at[slot]).wait()

        return finish

    got_spec = exchange(0, "freq", nq, q, lambda i: spec_ref.at[i], spec_all)
    got_sums = exchange(1, "freq", nq, q, lambda i: own_ref.at[i], sums_ref)

    got_spec()

    def widen(b, carry):
        block = spec_all[b].astype(jnp.float32)
        there = pl.ds(pl.multiple_of(b * pad, pad), cols)
        for h in range(width // LANES):
            flat[h, there, :] = block[:, h * LANES : (h + 1) * LANES]
        return carry

    lax.fori_loop(0, blocks, widen, 0)
    for j in range(cols):
        for h in range(width // LANES):
            rows[j * blocks : (j + 1) * blocks, h * LANES : (h + 1) * LANES] = flat[
                h, pl.ds(j, blocks, stride=pad), :
            ].astype(jnp.bfloat16)

    half = width // 2
    for c in range(triads // 256):
        lanes = slice(c * 256, (c + 1) * 256)
        at = lax.broadcasted_iota(jnp.int32, (width, 256), 0)

        def pick(row, shift):
            hot = jnp.where(at == triad_ref[row : row + 1, lanes] + shift, 1.0, 0.0)
            return hot.astype(jnp.bfloat16)

        hots = [pick(row, shift) for row in range(3) for shift in (0, half)]
        for j in range(0, cols, 2):
            here = slice(j * blocks, (j + 2) * blocks)
            k_re, k_im, l_re, l_im, s_re, s_im = [
                jnp.dot(rows[here, :], hot, preferred_element_type=jnp.float32) for hot in hots
            ]
            weight = weight_ref[here, :]
            weight = jnp.concatenate([weight, weight], axis=1)
            prod_re[here, lanes] = ((k_re * l_re - k_im * l_im) * weight).astype(jnp.bfloat16)
            prod_im[here, lanes] = ((k_re * l_im + k_im * l_re) * weight).astype(jnp.bfloat16)
            sum_re[here, lanes] = s_re.astype(jnp.bfloat16)
            sum_im[here, lanes] = s_im.astype(jnp.bfloat16)

    coef_ref[0] = jnp.ones((blocks, triads), jnp.float32)
    coef_ref[1] = jnp.zeros((blocks, triads), jnp.float32)

    for sweep in range(2):
        for g in range(groups):
            lanes = slice(g * LANES, (g + 1) * LANES)
            a_re, a_im = coef_ref[0, :, lanes], coef_ref[1, :, lanes]

            def column(j, carry):
                v_re, v_im = carry
                here = pl.ds(pl.multiple_of(j * blocks, blocks), blocks)
                s_re = sum_re[here, lanes].astype(jnp.float32)
                s_im = sum_im[here, lanes].astype(jnp.float32)
                f_re = jnp.sum(a_re * s_re - a_im * s_im, axis=0, keepdims=True)
                f_im = jnp.sum(a_re * s_im + a_im * s_re, axis=0, keepdims=True)
                p_re = prod_re[here, lanes].astype(jnp.float32)
                p_im = prod_im[here, lanes].astype(jnp.float32)
                return (v_re + (p_re * f_re + p_im * f_im), v_im + (p_re * f_im - p_im * f_re))

            zero = jnp.zeros((blocks, LANES), jnp.float32)
            v_re, v_im = lax.fori_loop(0, cols, column, (zero, zero))
            part[sweep, 0, :, lanes] = v_re
            part[sweep, 1, :, lanes] = v_im

        base = 2 + 4 * sweep
        exchange(
            base, "space", ne, e,
            lambda i: part.at[sweep, :, pl.ds(pl.multiple_of(i * per_e, per_e), per_e), :],
            part_in.at[sweep],
        )()
        total = jnp.sum(part_in[sweep], axis=0)
        for r in range(2):
            for b in range(per_e):
                for g in range(groups):
                    piece[sweep, (r * per_e + b) * groups + g] = total[
                        r, b : b + 1, g * LANES : (g + 1) * LANES
                    ]
        exchange(
            base + 1, "freq", nq, q, lambda i: piece.at[sweep, i], piece_in.at[sweep]
        )()
        mine[sweep] = jnp.sum(piece_in[sweep], axis=0)
        exchange(base + 2, "freq", nq, q, lambda i: mine.at[sweep], gathered.at[sweep])()
        exchange(base + 3, "space", ne, e, lambda i: gathered.at[sweep], spread.at[sweep])()

        def place(d, carry):
            for r in range(2):
                for g in range(groups):
                    block = jnp.concatenate(
                        [spread[sweep, d, (r * per_e + b) * groups + g] for b in range(per_e)], axis=0
                    )
                    there = pl.ds(pl.multiple_of(d * per_e, per_e), per_e)
                    coef_ref[r, there, g * LANES : (g + 1) * LANES] = block
            return carry

        lax.fori_loop(0, ne, place, 0)
        v_re, v_im = coef_ref[0], coef_ref[1]
        energy = jnp.sum(v_re * v_re + v_im * v_im, axis=0, keepdims=True) / blocks
        factor = lax.rsqrt(energy + 1e-05)
        coef_ref[0] = v_re * factor
        coef_ref[1] = v_im * factor

    got_sums()


def exchange_and_iterate(nq, ne, spec, own, weight, triad):
    blocks, cols, width = spec.shape
    triads = triad.shape[1]
    pieces = 2 * (blocks // ne) * (triads // LANES)
    assert pieces == nq
    f32, bf16 = jnp.float32, jnp.bfloat16
    vmem = pl.BlockSpec(memory_space=pltpu.VMEM)
    return pl.pallas_call(
        functools.partial(kernel, nq, ne),
        out_shape=(
            jax.ShapeDtypeStruct((2, blocks, triads), f32),
            jax.ShapeDtypeStruct(own.shape, bf16),
        ),
        in_specs=[vmem] * 4,
        out_specs=(vmem, vmem),
        scratch_shapes=[
            pltpu.VMEM((blocks, cols, width), bf16),
            pltpu.VMEM((width // LANES, blocks * 16, LANES), f32),
            pltpu.VMEM((cols * blocks, width), bf16),
            pltpu.VMEM((cols * blocks, triads), bf16),
            pltpu.VMEM((cols * blocks, triads), bf16),
            pltpu.VMEM((cols * blocks, triads), bf16),
            pltpu.VMEM((cols * blocks, triads), bf16),
            pltpu.VMEM((8, LANES), f32),
            pltpu.VMEM((2, 2, blocks, triads), f32),
            pltpu.VMEM((2, ne, 2, blocks // ne, triads), f32),
            pltpu.VMEM((2, pieces, 1, LANES), f32),
            pltpu.VMEM((2, nq, 1, LANES), f32),
            pltpu.VMEM((2, 1, LANES), f32),
            pltpu.VMEM((2, nq, 1, LANES), f32),
            pltpu.VMEM((2, ne, nq, 1, LANES), f32),
            pltpu.SemaphoreType.DMA((10,)),
            pltpu.SemaphoreType.DMA((10,)),
        ],
        compiler_params=pltpu.CompilerParams(
            collective_id=0, has_side_effects=True, vmem_limit_bytes=48 * 1024 * 1024
        ),
    )(spec, own, weight, triad)


def body(snapshots, point_weights, owner_map, triad_list):
    samples = snapshots.shape[1]
    points = snapshots.shape[3]
    columns = 3 * points
    frequencies = owner_map.shape[0]
    triad_count = triad_list.shape[0]
    nq, ne = lax.axis_size("freq"), lax.axis_size("space")
    triads_here = triad_count // nq
    slots = frequencies // nq
    per_slot = triads_here // slots
    mine = lax.axis_index("freq")
    table = make_table(samples, frequencies)
    data = snapshots.reshape(samples, columns)
    by_part = table.reshape(frequencies, 2, samples).transpose(1, 0, 2).reshape(2 * frequencies, samples)
    spec = lax.dot_general(
        data, by_part, (((0,), (1,)), ((), ())), preferred_element_type=jnp.float32
    ).astype(jnp.bfloat16)
    owned_table = select_rows(owner_map, table.reshape(frequencies, 2 * samples))
    own = jnp.dot(
        owned_table.astype(jnp.bfloat16).reshape(2 * frequencies, samples),
        data,
        preferred_element_type=jnp.float32,
    ).astype(jnp.bfloat16)
    cols = columns // nq
    weight = lax.dynamic_slice(jnp.tile(point_weights, 3), (mine * cols,), (cols,))
    weight = jnp.broadcast_to(weight[:, None, None], (cols, nq, LANES)).reshape(cols * nq, LANES)
    first, second = triad_list[:, 0], triad_list[:, 1]
    triad = jnp.stack([first, second, first + second])
    coef, sums = exchange_and_iterate(
        nq, ne, spec.reshape(nq, cols, 2 * frequencies), own.reshape(nq, 2 * slots, columns), weight, triad
    )
    coefficients = lax.dynamic_slice(coef, (0, 0, mine * triads_here), (2, nq, triads_here))
    coefficients = coefficients.transpose(2, 0, 1)
    sums = sums.reshape(nq, slots, 2, columns)
    sums_f = sums.astype(jnp.float32)
    power_map = jnp.sum((sums_f * sums_f).reshape(nq, slots, 6, points), axis=(0, 2)) / nq
    rounded = coefficients.astype(jnp.bfloat16).reshape(per_slot, slots, 2, nq)
    out = jnp.einsum("quxb,buyk->quxyk", rounded, sums, preferred_element_type=jnp.float32)
    mode_real = out[:, :, 0, 0] - out[:, :, 1, 1]
    mode_imag = out[:, :, 0, 1] + out[:, :, 1, 0]
    modes = jnp.stack([mode_real, mode_imag], axis=2) / math.sqrt(nq)
    return (power_map, coefficients, modes.reshape(triads_here, 2, 3, points))


def solution(mesh):
    placed = (P("freq", None, None, "space"), P("space"), P(), P())
    return jax.shard_map(
        body,
        mesh=mesh,
        in_specs=placed,
        out_specs=(P("freq", "space"), P("freq", None, None), P("freq", None, None, "space")),
        check_vma=False,
    )
```

time: 222 us -> 117 us (0.53)
  blocking collectives: 159 us -> 0 us
  Pallas kernels: 0 us -> 108 us
  local copies, waits for them, and re-layouts: 19.8 us -> 5.36 us
  other arithmetic: 15.1 us -> 1.61 us
  starting transfers between devices: 12.9 us -> 0 us
  waiting for transfers between devices: 7.66 us -> 0 us
  matrix products: 4.81 us -> 0.98 us
    all_to_all x1 -> x0, blocking collectives: 159 us -> none  [body(): lax.all_to_all(packet, 'freq', split_axis=0, concat_axis=0, tiled=True)]
    pallas_call x0 -> x1, Pallas kernels: none -> 108 us  [exchange_and_iterate(): pl.pallas_call(functools.partial(kernel, nq, ne), out_shape=(jax.ShapeDty...]
    all_to_all x2 -> x0, starting transfers between devices: 12.9 us -> none  [sum_over_space(): lax.all_to_all(spread, 'space', split_axis=0, concat_axis=0, tiled=True)]
    all_to_all x2 -> x0, waiting for transfers between devices: 7.66 us -> none  [sum_over_space(): lax.all_to_all(spread, 'space', split_axis=0, concat_axis=0, tiled=True)]
    unnamed x21 -> x11, local copies, waits for them, and re-layouts: 11.2 us -> 4.24 us
    reduce_sum x7 -> x2, other arithmetic: 5.49 us -> 0.26 us  [body(): jnp.sum((sums_f * sums_f).reshape(nq, slots, 6, points), axis=(0, 2)) / nq]
    convert_element_type x2, other arithmetic: 4.18 us -> 0.11 us  [the longest x1 0.09 us: body(): rounded = coefficients.astype(jnp.bfloat16).reshape(per_slot, slots, 2, nq)]
    dot_general x3 -> x1, matrix products: 3.95 us -> 0.22 us  [select_rows(): return jnp.dot(hot, rows, preferred_element_type=jnp.float32)]
  transfers between devices with their start and end apart: 2 -> 0, of which waited for: 2 -> 0; matrix products, arithmetic and copies ran while one was open for 1% -> 0% of each run, Pallas kernels for 0% -> 0%
where the time goes in v2:
time: 117 us
  Pallas kernels  108 us (92%)
  local copies, waits for them, and re-layouts  5.36 us (5%)
  other arithmetic  1.61 us (1%)
    pallas_call x1, Pallas kernels, exchange_and_iterate(): pl.pallas_call(functools.partial(kernel, nq, ne), out_shape=(jax.ShapeDty...  108 us
    unnamed x11, local copies, waits for them, and re-layouts  4.24 us

profile of v2, /device:TPU:1, one launch (start us, length us, event | category | flops | bytes accessed | tf_op | source)
XLA Modules:
  0.0 117.1 jit_solution(15794499369906283870)
XLA Ops:
  0.6 0.0 copy-start.1
  0.7 0.6 copy-done.1
  1.3 0.0 copy-start.2
  1.3 0.7 copy-done.2
  2.0 0.1 dynamic_slice.6
  2.1 0.1 broadcast_in_dim.6
  2.2 0.1 broadcast_in_dim.7
  2.3 0.6 cosine_multiply_fusion
  2.8 0.1 copy.32
  3.0 0.0 copy-start.3
  3.0 0.6 copy-done.3
  3.6 0.2 convolution_convert_fusion.2
  3.9 0.0 copy-start
  3.9 0.2 broadcast_in_dim.8.weight_ref
  4.1 0.8 copy-done
  4.9 0.2 copy.30
  5.0 0.3 convolution_convert_fusion
  5.3 0.3 fusion
  5.6 0.2 copy.31
  5.8 0.1 reshape.224.own_ref
  5.9 0.1 reshape.222.spec_ref
  6.0 108.3 %shard_map.67 = (f32[2,64,512]{2,1,0:T(8,128)S(1)}, bf16[64,4,768]{2,1,0:T(4,128)(2,1)S(1)}) custom-call(bf16[64,12,256]{2,1,0:T(8,128)(2,1)S(1)} %reshape.222.spec_ref, bf16[64,4,768]{2,1,0:T(4,128)(2,1)S(1)} %reshape.224.own_ref, f32[768,128]{1,0:T(8,128)S(1)} %broadcast_in_dim.8.weight_ref, s32[3,512]{1,0:T(4,128)S(1)} %pad_add_fusion.triad_ref), custom_call_target="tpu_custom_call" | custom-call | tf_op jit(solution)/shard_map/pallas_call | solution.py:194
  114.4 0.1 fusion.10
  114.5 0.1 copy.33
  114.5 0.7 copy.38
  115.2 0.2 multiply_reduce_fusion
  115.5 0.2 convolution_bitcast_fusion
  115.8 0.6 broadcast_multiply_fusion
  116.5 0.7 copy.39
  (17 shorter events, 0.3 us)
Async XLA Ops:
  0.6 0.7 copy-start.1
  1.3 0.7 copy-start.2
  3.0 0.7 copy-start.3
  3.9 1.0 copy-start

commit v3 on v2

--- a/solution.py
+++ b/solution.py
@@ -26,20 +26,27 @@
     return jnp.dot(hot, rows, preferred_element_type=jnp.float32)
 
 
+def normalized(vec_real, vec_imag):
+    energy = jnp.mean(vec_real * vec_real + vec_imag * vec_imag, axis=-1, keepdims=True)
+    factor = lax.rsqrt(energy + 1e-05)
+    return (vec_real * factor, vec_imag * factor)
+
+
 MESH = pl.DeviceIdType.MESH
 LANES = 128
 
 
 def kernel(
     nq, ne, spec_ref, own_ref, weight_ref, triad_ref,
-    coef_ref, sums_ref,
+    last_ref, sums_ref,
     spec_all, flat, rows, prod_re, prod_im, sum_re, sum_im, field,
-    part, part_in, piece, piece_in, mine, gathered, spread,
+    coef_ref, part, part_in, piece, piece_in, mine, gathered, spread,
     send_sem, recv_sem,
 ):
     q = lax.axis_index("freq")
     e = lax.axis_index("space")
-    blocks, cols, width = spec_ref.shape
+    blocks, bands, band, width = spec_ref.shape
+    cols = bands * band
     pad = flat.shape[1] // blocks
     triads = triad_ref.shape[1]
     per_e = blocks // ne
@@ -80,15 +87,14 @@
         return finish
 
     got_spec = exchange(0, "freq", nq, q, lambda i: spec_ref.at[i], spec_all)
-    got_sums = exchange(1, "freq", nq, q, lambda i: own_ref.at[i], sums_ref)
-
     got_spec()
 
     def widen(b, carry):
-        block = spec_all[b].astype(jnp.float32)
-        there = pl.ds(pl.multiple_of(b * pad, pad), cols)
-        for h in range(width // LANES):
-            flat[h, there, :] = block[:, h * LANES : (h + 1) * LANES]
+        for k in range(bands):
+            block = spec_all[b, k].astype(jnp.float32)
+            there = pl.ds(b * pad + k * band, band)
+            for h in range(width // LANES):
+                flat[h, there, :] = block[:, h * LANES : (h + 1) * LANES]
         return carry
 
     lax.fori_loop(0, blocks, widen, 0)
@@ -151,24 +157,40 @@
             part_in.at[sweep],
         )()
         total = jnp.sum(part_in[sweep], axis=0)
-        for r in range(2):
-            for b in range(per_e):
-                for g in range(groups):
-                    piece[sweep, (r * per_e + b) * groups + g] = total[
-                        r, b : b + 1, g * LANES : (g + 1) * LANES
-                    ]
+        if sweep == 0:
+            for r in range(2):
+                for b in range(per_e):
+                    for g in range(groups):
+                        piece[sweep, (r * per_e + b) * groups + g] = total[
+                            r, b : b + 1, g * LANES : (g + 1) * LANES
+                        ]
+        else:
+            stack = jnp.concatenate(
+                [total[r, :, g * LANES : (g + 1) * LANES] for g in range(groups) for r in range(2)], axis=0
+            )
+            blank = jnp.zeros_like(stack)
+            even = jnp.concatenate([stack, blank], axis=0).T
+            odd = jnp.concatenate([blank, stack], axis=0).T
+            by_owner = even[:nq] + odd[nq:]
+            for i in range(nq):
+                piece[sweep, i] = by_owner[i : i + 1]
         exchange(
             base + 1, "freq", nq, q, lambda i: piece.at[sweep, i], piece_in.at[sweep]
         )()
         mine[sweep] = jnp.sum(piece_in[sweep], axis=0)
-        exchange(base + 2, "freq", nq, q, lambda i: mine.at[sweep], gathered.at[sweep])()
-        exchange(base + 3, "space", ne, e, lambda i: gathered.at[sweep], spread.at[sweep])()
+        if sweep == 1:
+            exchange(base + 3, "space", ne, e, lambda i: mine.at[sweep], last_ref)()
+            break
+        got_mine = exchange(base + 2, "freq", nq, q, lambda i: mine.at[sweep], gathered)
+        got_sums = exchange(1, "freq", nq, q, lambda i: own_ref.at[i], sums_ref)
+        got_mine()
+        exchange(base + 3, "space", ne, e, lambda i: gathered, spread)()
 
         def place(d, carry):
             for r in range(2):
                 for g in range(groups):
                     block = jnp.concatenate(
-                        [spread[sweep, d, (r * per_e + b) * groups + g] for b in range(per_e)], axis=0
+                        [spread[d, (r * per_e + b) * groups + g] for b in range(per_e)], axis=0
                     )
                     there = pl.ds(pl.multiple_of(d * per_e, per_e), per_e)
                     coef_ref[r, there, g * LANES : (g + 1) * LANES] = block
@@ -185,22 +207,23 @@
 
 
 def exchange_and_iterate(nq, ne, spec, own, weight, triad):
-    blocks, cols, width = spec.shape
+    blocks, bands, band, width = spec.shape
+    cols = bands * band
     triads = triad.shape[1]
     pieces = 2 * (blocks // ne) * (triads // LANES)
-    assert pieces == nq
+    assert pieces == nq and LANES == 2 * nq and triads == 8 * nq
     f32, bf16 = jnp.float32, jnp.bfloat16
     vmem = pl.BlockSpec(memory_space=pltpu.VMEM)
     return pl.pallas_call(
         functools.partial(kernel, nq, ne),
         out_shape=(
-            jax.ShapeDtypeStruct((2, blocks, triads), f32),
+            jax.ShapeDtypeStruct((ne, 1, LANES), f32),
             jax.ShapeDtypeStruct(own.shape, bf16),
         ),
         in_specs=[vmem] * 4,
         out_specs=(vmem, vmem),
         scratch_shapes=[
-            pltpu.VMEM((blocks, cols, width), bf16),
+            pltpu.VMEM((blocks, bands, band, width), bf16),
             pltpu.VMEM((width // LANES, blocks * 16, LANES), f32),
             pltpu.VMEM((cols * blocks, width), bf16),
             pltpu.VMEM((cols * blocks, triads), bf16),
@@ -208,13 +231,14 @@
             pltpu.VMEM((cols * blocks, triads), bf16),
             pltpu.VMEM((cols * blocks, triads), bf16),
             pltpu.VMEM((8, LANES), f32),
+            pltpu.VMEM((2, blocks, triads), f32),
             pltpu.VMEM((2, 2, blocks, triads), f32),
             pltpu.VMEM((2, ne, 2, blocks // ne, triads), f32),
             pltpu.VMEM((2, pieces, 1, LANES), f32),
             pltpu.VMEM((2, nq, 1, LANES), f32),
             pltpu.VMEM((2, 1, LANES), f32),
-            pltpu.VMEM((2, nq, 1, LANES), f32),
-            pltpu.VMEM((2, ne, nq, 1, LANES), f32),
+            pltpu.VMEM((nq, 1, LANES), f32),
+            pltpu.VMEM((ne, nq, 1, LANES), f32),
             pltpu.SemaphoreType.DMA((10,)),
             pltpu.SemaphoreType.DMA((10,)),
         ],
@@ -252,11 +276,13 @@
     weight = jnp.broadcast_to(weight[:, None, None], (cols, nq, LANES)).reshape(cols * nq, LANES)
     first, second = triad_list[:, 0], triad_list[:, 1]
     triad = jnp.stack([first, second, first + second])
-    coef, sums = exchange_and_iterate(
-        nq, ne, spec.reshape(nq, cols, 2 * frequencies), own.reshape(nq, 2 * slots, columns), weight, triad
+    triad = triad.reshape(3, nq, triads_here).transpose(0, 2, 1).reshape(3, triad_count)
+    last, sums = exchange_and_iterate(
+        nq, ne, spec.reshape(nq, cols // 4, 4, 2 * frequencies), own.reshape(nq, 2 * slots, columns), weight, triad
     )
-    coefficients = lax.dynamic_slice(coef, (0, 0, mine * triads_here), (2, nq, triads_here))
-    coefficients = coefficients.transpose(2, 0, 1)
+    vec = last.reshape(ne, 2, triads_here // 2, 2, nq // ne).transpose(2, 1, 3, 0, 4)
+    vec = vec.reshape(triads_here, 2, nq)
+    coefficients = jnp.stack(normalized(vec[:, 0], vec[:, 1]), axis=1)
     sums = sums.reshape(nq, slots, 2, columns)
     sums_f = sums.astype(jnp.float32)
     power_map = jnp.sum((sums_f * sums_f).reshape(nq, slots, 6, points), axis=(0, 2)) / nq

time: 117 us -> 101 us (0.86)
  Pallas kernels: 108 us -> 90.8 us
    pallas_call x1, Pallas kernels: 108 us -> 90.8 us  [exchange_and_iterate(): pl.pallas_call(functools.partial(kernel, nq, ne), out_shape=(jax.ShapeDty...]
where the time goes in v3:
time: 101 us
  Pallas kernels  90.8 us (90%)
  local copies, waits for them, and re-layouts  5.85 us (6%)
  other arithmetic  2.38 us (2%)
    pallas_call x1, Pallas kernels, exchange_and_iterate(): pl.pallas_call(functools.partial(kernel, nq, ne), out_shape=(jax.ShapeDty...  90.8 us
    unnamed x11, local copies, waits for them, and re-layouts  3.56 us

profile of v3, /device:TPU:1, one launch (start us, length us, event | category | flops | bytes accessed | tf_op | source)
XLA Modules:
  0.0 100.8 jit_solution(12123120313527668291)
XLA Ops:
  0.6 0.0 copy-start
  0.7 0.6 cosine_multiply_fusion
  1.3 0.4 copy-done
  1.6 0.2 copy.37
  1.8 0.3 fusion
  2.1 0.2 copy.38
  2.3 0.1 reshape.264.spec_ref
  2.4 0.1 copy.39
  2.5 0.0 copy-start.3
  2.5 0.6 copy-done.3
  3.2 0.2 convolution_convert_fusion.2
  3.5 0.3 convolution_convert_fusion
  3.8 0.0 copy-start.2
  3.8 0.1 reshape.266.own_ref
  3.9 0.6 copy-done.2
  4.5 0.1 dynamic_slice.3
  4.5 0.1 broadcast_in_dim.6
  4.6 0.1 broadcast_in_dim.7
  4.7 0.0 copy-start.1
  4.7 0.2 broadcast_in_dim.8.weight_ref
  4.8 0.5 copy-done.1
  5.4 0.1 stack.30
  5.5 0.1 stack.31
  5.6 0.1 copy.42
  5.7 0.1 copy.41
  5.7 0.1 copy.40
  5.8 0.1 reshape.267.triad_ref
  5.9 90.8 %shard_map.67 = (f32[8,1,128]{2,1,0:T(1,128)S(1)}, bf16[64,4,768]{2,1,0:T(4,128)(2,1)S(1)}) custom-call(bf16[64,3,4,256]{3,2,1,0:T(4,128)(2,1)S(1)} %reshape.264.spec_ref, bf16[64,4,768]{2,1,0:T(4,128)(2,1)S(1)} %reshape.266.own_ref, f32[768,128]{1,0:T(8,128)S(1)} %broadcast_in_dim.8.weight_ref, s32[3,512]{1,0:T(4,128)S(1)} %reshape.267.triad_ref), custom_call_target="tpu_custom_call" | custom-call | tf_op jit(solution)/shard_map/pallas_call | solution.py:217
  96.6 0.2 multiply_reduce_fusion
  96.9 0.6 broadcast_multiply_fusion
  97.5 0.5 broadcast.184
  98.0 0.7 reduce.14
  98.7 0.1 reshape.268
  98.9 0.1 reshape.269
  98.9 0.1 add_reduce_fusion
  99.1 0.1 fusion.11
  99.1 0.6 copy.49
  99.8 0.2 convolution_bitcast_fusion
  100.2 0.7 copy.50
  (22 shorter events, 0.4 us)
Async XLA Ops:
  0.6 1.0 copy-start
  2.5 0.7 copy-start.3
  3.8 0.7 copy-start.2
  4.7 0.7 copy-start.1

commit v4 on v3

--- a/solution.py
+++ b/solution.py
@@ -38,8 +38,8 @@
 
 def kernel(
     nq, ne, spec_ref, own_ref, weight_ref, triad_ref,
-    last_ref, sums_ref,
-    spec_all, flat, rows, prod_re, prod_im, sum_re, sum_im, field,
+    last_ref, sums_ref, power_ref,
+    weight_rows, spec_all, flat, rows, prod_re, prod_im, sum_re, sum_im, field,
     coef_ref, part, part_in, piece, piece_in, mine, gathered, spread,
     send_sem, recv_sem,
 ):
@@ -54,18 +54,32 @@
 
     barrier = pltpu.get_barrier_semaphore()
 
+    ring = 16
+
+    def far_first(k, count):
+        return (count // 2 + (1 - 2 * (k % 2)) * ((k + 1) // 2)) % count
+
     def others(axis, count, index, act):
-        def step(i, carry):
-            act({axis: lax.rem(index + i, count)}, lax.rem(index + i, count))
+        def step(k, carry):
+            if axis == "freq":
+                outer = count // ring
+                far_z, far_y = far_first(k // outer, ring), far_first(k % outer, outer)
+                i = (index // ring + far_y) % outer * ring + (index + far_z) % ring
+            else:
+                i = (index + far_first(k, count)) % count
+            act({axis: i}, i)
             return carry
 
-        lax.fori_loop(1, count, step, 0)
+        lax.fori_loop(0, count - 1, step, 0)
 
     def greet(device, _):
         pl.semaphore_signal(barrier, inc=1, device_id=device, device_id_type=MESH)
 
     others("freq", nq, q, greet)
     others("space", ne, e, greet)
+    for j in range(cols):
+        value = weight_ref[(q * cols + j) % weight_ref.shape[0]]
+        weight_rows[j * blocks : (j + 1) * blocks, :] = jnp.full((blocks, LANES), value)
     pl.semaphore_wait(barrier, nq + ne - 2)
 
     def exchange(slot, axis, count, index, source, target):
@@ -119,7 +133,7 @@
             k_re, k_im, l_re, l_im, s_re, s_im = [
                 jnp.dot(rows[here, :], hot, preferred_element_type=jnp.float32) for hot in hots
             ]
-            weight = weight_ref[here, :]
+            weight = weight_rows[here, :]
             weight = jnp.concatenate([weight, weight], axis=1)
             prod_re[here, lanes] = ((k_re * l_re - k_im * l_im) * weight).astype(jnp.bfloat16)
             prod_im[here, lanes] = ((k_re * l_im + k_im * l_re) * weight).astype(jnp.bfloat16)
@@ -174,9 +188,23 @@
             by_owner = even[:nq] + odd[nq:]
             for i in range(nq):
                 piece[sweep, i] = by_owner[i : i + 1]
-        exchange(
+        got_piece = exchange(
             base + 1, "freq", nq, q, lambda i: piece.at[sweep, i], piece_in.at[sweep]
-        )()
+        )
+        if sweep == 1:
+            got_sums()
+
+            def energy_of(b, total):
+                values = sums_ref[b].astype(jnp.float32)
+                return total + values * values
+
+            energy = lax.fori_loop(0, blocks, energy_of, jnp.zeros(sums_ref.shape[1:], jnp.float32))
+            points = power_ref.shape[1]
+            for slot in range(power_ref.shape[0]):
+                pair = energy[2 * slot : 2 * slot + 1] + energy[2 * slot + 1 : 2 * slot + 2]
+                pair = pair[:, :points] + pair[:, points : 2 * points] + pair[:, 2 * points :]
+                power_ref[slot : slot + 1, :] = pair / blocks
+        got_piece()
         mine[sweep] = jnp.sum(piece_in[sweep], axis=0)
         if sweep == 1:
             exchange(base + 3, "space", ne, e, lambda i: mine.at[sweep], last_ref)()
@@ -202,8 +230,6 @@
         factor = lax.rsqrt(energy + 1e-05)
         coef_ref[0] = v_re * factor
         coef_ref[1] = v_im * factor
-
-    got_sums()
 
 
 def exchange_and_iterate(nq, ne, spec, own, weight, triad):
@@ -219,10 +245,12 @@
         out_shape=(
             jax.ShapeDtypeStruct((ne, 1, LANES), f32),
             jax.ShapeDtypeStruct(own.shape, bf16),
+            jax.ShapeDtypeStruct((own.shape[1] // 2, own.shape[2] // 3), f32),
         ),
-        in_specs=[vmem] * 4,
-        out_specs=(vmem, vmem),
+        in_specs=[vmem, vmem, pl.BlockSpec(memory_space=pltpu.SMEM), vmem],
+        out_specs=(vmem, vmem, vmem),
         scratch_shapes=[
+            pltpu.VMEM((cols * blocks, LANES), f32),
             pltpu.VMEM((blocks, bands, band, width), bf16),
             pltpu.VMEM((width // LANES, blocks * 16, LANES), f32),
             pltpu.VMEM((cols * blocks, width), bf16),
@@ -272,20 +300,16 @@
         preferred_element_type=jnp.float32,
     ).astype(jnp.bfloat16)
     cols = columns // nq
-    weight = lax.dynamic_slice(jnp.tile(point_weights, 3), (mine * cols,), (cols,))
-    weight = jnp.broadcast_to(weight[:, None, None], (cols, nq, LANES)).reshape(cols * nq, LANES)
     first, second = triad_list[:, 0], triad_list[:, 1]
     triad = jnp.stack([first, second, first + second])
     triad = triad.reshape(3, nq, triads_here).transpose(0, 2, 1).reshape(3, triad_count)
-    last, sums = exchange_and_iterate(
-        nq, ne, spec.reshape(nq, cols // 4, 4, 2 * frequencies), own.reshape(nq, 2 * slots, columns), weight, triad
+    last, sums, power_map = exchange_and_iterate(
+        nq, ne, spec.reshape(nq, cols // 4, 4, 2 * frequencies), own.reshape(nq, 2 * slots, columns), point_weights, triad
     )
     vec = last.reshape(ne, 2, triads_here // 2, 2, nq // ne).transpose(2, 1, 3, 0, 4)
     vec = vec.reshape(triads_here, 2, nq)
     coefficients = jnp.stack(normalized(vec[:, 0], vec[:, 1]), axis=1)
     sums = sums.reshape(nq, slots, 2, columns)
-    sums_f = sums.astype(jnp.float32)
-    power_map = jnp.sum((sums_f * sums_f).reshape(nq, slots, 6, points), axis=(0, 2)) / nq
     rounded = coefficients.astype(jnp.bfloat16).reshape(per_slot, slots, 2, nq)
     out = jnp.einsum("quxb,buyk->quxyk", rounded, sums, preferred_element_type=jnp.float32)
     mode_real = out[:, :, 0, 0] - out[:, :, 1, 1]

time: 101 us -> 96.7 us (0.957)
  Pallas kernels: 90.8 us -> 86.9 us
    pallas_call x1, Pallas kernels: 90.8 us -> 86.9 us  [exchange_and_iterate(): pl.pallas_call(functools.partial(kernel, nq, ne), out_shape=(jax.ShapeDty...]
    unnamed x11 -> x12, local copies, waits for them, and re-layouts: 3.56 us -> 4.22 us
where the time goes in v4:
time: 96.7 us; the launch traced here: 96.4 us
  Pallas kernels  86.9 us (90%)
  local copies, waits for them, and re-layouts  6.12 us (6%)
  other arithmetic  1.53 us (2%)
  matrix products  0.98 us (1%)
    pallas_call x1, Pallas kernels, exchange_and_iterate(): pl.pallas_call(functools.partial(kernel, nq, ne), out_shape=(jax.ShapeDty...  86.9 us
    unnamed x12, local copies, waits for them, and re-layouts  4.22 us

profile of v4, /device:TPU:1, one launch (start us, length us, event | category | flops | bytes accessed | tf_op | source)
XLA Modules:
  0.0 96.4 jit_solution(16600995580313499882)
XLA Ops:
  0.6 0.0 copy-start.1
  0.7 0.6 cosine_multiply_fusion
  1.3 0.4 copy-done.1
  1.6 0.2 copy.37
  1.8 0.3 fusion
  2.1 0.2 copy.38
  2.3 0.1 reshape.257.spec_ref
  2.4 0.1 copy.39
  2.5 0.0 copy-start.3
  2.5 0.6 copy-done.3
  3.2 0.2 convolution_convert_fusion.2
  3.5 0.3 convolution_convert_fusion
  3.8 0.0 copy-start.2
  3.8 0.1 reshape.259.own_ref
  3.9 0.6 copy-done.2
  4.5 0.1 stack.30
  4.6 0.1 stack.31
  4.7 0.1 copy.42
  4.7 0.1 copy.41
  4.8 0.1 copy.40
  4.9 0.0 copy-start
  4.9 0.1 reshape.260.triad_ref
  5.0 0.6 copy-done
  5.6 86.9 %shard_map.67 = (f32[8,1,128]{2,1,0:T(1,128)S(1)}, bf16[64,4,768]{2,1,0:T(4,128)(2,1)S(1)}, f32[2,256]{1,0:T(2,128)S(1)}) custom-call(bf16[64,3,4,256]{3,2,1,0:T(4,128)(2,1)S(1)} %reshape.257.spec_ref, bf16[64,4,768]{2,1,0:T(4,128)(2,1)S(1)} %reshape.259.own_ref, f32[256]{0:T(256)S(1)} %copy-done, s32[3,512]{1,0:T(4,128)S(1)} %reshape.260.triad_ref), custom_call_target="tpu_custom_call" | custom-call | tf_op jit(solution)/shard_map/pallas_call | solution.py:243
  92.5 0.5 broadcast.179
  93.0 0.7 reduce.12
  93.7 0.1 reshape.261
  93.9 0.1 reshape.262
  94.0 0.1 add_reduce_fusion
  94.1 0.1 fusion.11
  94.2 0.6 copy.49
  94.9 0.2 convolution_bitcast_fusion
  95.2 0.7 copy.50
  95.8 0.6 copy.55
  (18 shorter events, 0.4 us)
Async XLA Ops:
  0.6 1.0 %copy-start.1 = (bf16[1,256,3,256]{3,1,2,0:T(8,128)(2,1)S(1)}, bf16[1,256,3,256]{3,1,2,0:T(8,128)(2,1)}, u32[]{:S(2)}) copy-start(bf16[1,256,3,256]{3,1,2,0:T(8,128)(2,1)} %param.4) | copy-start | bytes 1179652
  2.5 0.7 copy-start.3
  3.8 0.7 copy-start.2
  4.9 0.7 copy-start

commit v5 on v4

--- a/solution.py
+++ b/solution.py
@@ -26,12 +26,6 @@
     return jnp.dot(hot, rows, preferred_element_type=jnp.float32)
 
 
-def normalized(vec_real, vec_imag):
-    energy = jnp.mean(vec_real * vec_real + vec_imag * vec_imag, axis=-1, keepdims=True)
-    factor = lax.rsqrt(energy + 1e-05)
-    return (vec_real * factor, vec_imag * factor)
-
-
 MESH = pl.DeviceIdType.MESH
 LANES = 128
 
@@ -41,7 +35,7 @@
     last_ref, sums_ref, power_ref,
     weight_rows, spec_all, flat, rows, prod_re, prod_im, sum_re, sum_im, field,
     coef_ref, part, part_in, piece, piece_in, mine, gathered, spread,
-    send_sem, recv_sem,
+    near_sem, send_sem, recv_sem,
 ):
     q = lax.axis_index("freq")
     e = lax.axis_index("space")
@@ -72,15 +66,26 @@
 
         lax.fori_loop(0, count - 1, step, 0)
 
+    def row(far_y, far_z):
+        rows_y = nq // ring
+        return {"freq": (q // ring + far_y) % rows_y * ring + (q % ring + far_z) % ring}
+
     def greet(device, _):
         pl.semaphore_signal(barrier, inc=1, device_id=device, device_id_type=MESH)
 
-    others("freq", nq, q, greet)
     others("space", ne, e, greet)
+    for far_y in range(1, nq // ring):
+        greet(row(far_y, 0), None)
+    for far_z in (1, ring - 1):
+        greet(row(0, far_z), None)
     for j in range(cols):
         value = weight_ref[(q * cols + j) % weight_ref.shape[0]]
         weight_rows[j * blocks : (j + 1) * blocks, :] = jnp.full((blocks, LANES), value)
-    pl.semaphore_wait(barrier, nq + ne - 2)
+    pl.semaphore_wait(barrier, ne - 1 + nq // ring - 1 + 2)
+    for k, far_z in enumerate((1, 1, 2, 4)):
+        for other in (far_z, ring - far_z):
+            pl.semaphore_signal(near_sem.at[k], inc=1, device_id=row(0, other), device_id_type=MESH)
+        pl.semaphore_wait(near_sem.at[k], 2)
 
     def exchange(slot, axis, count, index, source, target):
         def act(device, i):
@@ -144,6 +149,8 @@
     coef_ref[1] = jnp.zeros((blocks, triads), jnp.float32)
 
     for sweep in range(2):
+        base = 2 + 7 * sweep
+        got_parts = []
         for g in range(groups):
             lanes = slice(g * LANES, (g + 1) * LANES)
             a_re, a_im = coef_ref[0, :, lanes], coef_ref[1, :, lanes]
@@ -161,26 +168,29 @@
 
             zero = jnp.zeros((blocks, LANES), jnp.float32)
             v_re, v_im = lax.fori_loop(0, cols, column, (zero, zero))
-            part[sweep, 0, :, lanes] = v_re
-            part[sweep, 1, :, lanes] = v_im
-
-        base = 2 + 4 * sweep
-        exchange(
-            base, "space", ne, e,
-            lambda i: part.at[sweep, :, pl.ds(pl.multiple_of(i * per_e, per_e), per_e), :],
-            part_in.at[sweep],
-        )()
-        total = jnp.sum(part_in[sweep], axis=0)
+            part[sweep, g, 0] = v_re
+            part[sweep, g, 1] = v_im
+            got_parts.append(
+                exchange(
+                    base + g, "space", ne, e,
+                    lambda i: part.at[sweep, g, :, pl.ds(pl.multiple_of(i * per_e, per_e), per_e), :],
+                    part_in.at[sweep, g],
+                )
+            )
+
+        for got_part in got_parts:
+            got_part()
+        totals = [jnp.sum(part_in[sweep, g], axis=0) for g in range(groups)]
         if sweep == 0:
             for r in range(2):
                 for b in range(per_e):
                     for g in range(groups):
-                        piece[sweep, (r * per_e + b) * groups + g] = total[
-                            r, b : b + 1, g * LANES : (g + 1) * LANES
+                        piece[sweep, (r * per_e + b) * groups + g] = totals[g][
+                            r, b : b + 1
                         ]
         else:
             stack = jnp.concatenate(
-                [total[r, :, g * LANES : (g + 1) * LANES] for g in range(groups) for r in range(2)], axis=0
+                [totals[g][r] for g in range(groups) for r in range(2)], axis=0
             )
             blank = jnp.zeros_like(stack)
             even = jnp.concatenate([stack, blank], axis=0).T
@@ -189,7 +199,7 @@
             for i in range(nq):
                 piece[sweep, i] = by_owner[i : i + 1]
         got_piece = exchange(
-            base + 1, "freq", nq, q, lambda i: piece.at[sweep, i], piece_in.at[sweep]
+            base + 4, "freq", nq, q, lambda i: piece.at[sweep, i], piece_in.at[sweep]
         )
         if sweep == 1:
             got_sums()
@@ -207,12 +217,25 @@
         got_piece()
         mine[sweep] = jnp.sum(piece_in[sweep], axis=0)
         if sweep == 1:
-            exchange(base + 3, "space", ne, e, lambda i: mine.at[sweep], last_ref)()
+            exchange(base + 6, "space", ne, e, lambda i: mine.at[sweep], last_ref)()
+            values = jnp.concatenate([last_ref[i] for i in range(ne)], axis=0)
+            square = jnp.sum(values * values, axis=0, keepdims=True)
+            share = 2 * per_e
+            here = lax.broadcasted_iota(jnp.int32, (LANES, LANES), 0) // share
+            there = lax.broadcasted_iota(jnp.int32, (LANES, LANES), 1) // share
+            same = jnp.where(here == there, 1.0, 0.0)
+            energy = jnp.dot(
+                jnp.broadcast_to(square, (ne, LANES)), same,
+                precision=lax.Precision.HIGHEST, preferred_element_type=jnp.float32,
+            )
+            values = values * lax.rsqrt(energy / blocks + 1e-05)
+            for i in range(ne):
+                last_ref[i] = values[i : i + 1]
             break
-        got_mine = exchange(base + 2, "freq", nq, q, lambda i: mine.at[sweep], gathered)
+        got_mine = exchange(base + 5, "freq", nq, q, lambda i: mine.at[sweep], gathered)
         got_sums = exchange(1, "freq", nq, q, lambda i: own_ref.at[i], sums_ref)
         got_mine()
-        exchange(base + 3, "space", ne, e, lambda i: gathered, spread)()
+        exchange(base + 6, "space", ne, e, lambda i: gathered, spread)()
 
         def place(d, carry):
             for r in range(2):
@@ -260,15 +283,16 @@
             pltpu.VMEM((cols * blocks, triads), bf16),
             pltpu.VMEM((8, LANES), f32),
             pltpu.VMEM((2, blocks, triads), f32),
-            pltpu.VMEM((2, 2, blocks, triads), f32),
-            pltpu.VMEM((2, ne, 2, blocks // ne, triads), f32),
+            pltpu.VMEM((2, triads // LANES, 2, blocks, LANES), f32),
+            pltpu.VMEM((2, triads // LANES, ne, 2, blocks // ne, LANES), f32),
             pltpu.VMEM((2, pieces, 1, LANES), f32),
             pltpu.VMEM((2, nq, 1, LANES), f32),
             pltpu.VMEM((2, 1, LANES), f32),
             pltpu.VMEM((nq, 1, LANES), f32),
             pltpu.VMEM((ne, nq, 1, LANES), f32),
-            pltpu.SemaphoreType.DMA((10,)),
-            pltpu.SemaphoreType.DMA((10,)),
+            pltpu.SemaphoreType.REGULAR((4,)),
+            pltpu.SemaphoreType.DMA((16,)),
+            pltpu.SemaphoreType.DMA((16,)),
         ],
         compiler_params=pltpu.CompilerParams(
             collective_id=0, has_side_effects=True, vmem_limit_bytes=48 * 1024 * 1024
@@ -307,8 +331,7 @@
         nq, ne, spec.reshape(nq, cols // 4, 4, 2 * frequencies), own.reshape(nq, 2 * slots, columns), point_weights, triad
     )
     vec = last.reshape(ne, 2, triads_here // 2, 2, nq // ne).transpose(2, 1, 3, 0, 4)
-    vec = vec.reshape(triads_here, 2, nq)
-    coefficients = jnp.stack(normalized(vec[:, 0], vec[:, 1]), axis=1)
+    coefficients = vec.reshape(triads_here, 2, nq)
     sums = sums.reshape(nq, slots, 2, columns)
     rounded = coefficients.astype(jnp.bfloat16).reshape(per_slot, slots, 2, nq)
     out = jnp.einsum("quxb,buyk->quxyk", rounded, sums, preferred_element_type=jnp.float32)

time: 96.7 us -> 98.4 us (1.018)
  Pallas kernels: 86.9 us -> 88.7 us
    pallas_call x1, Pallas kernels: 86.9 us -> 88.7 us  [exchange_and_iterate(): pl.pallas_call(functools.partial(kernel, nq, ne), out_shape=(jax.ShapeDty...]
    unnamed x12 -> x11, local copies, waits for them, and re-layouts: 4.22 us -> 3.61 us
where the time goes in v5:
time: 98.4 us; the launch traced here: 98.1 us
  Pallas kernels  88.7 us (90%)
  local copies, waits for them, and re-layouts  6.21 us (6%)
  other arithmetic  1.35 us (1%)
    pallas_call x1, Pallas kernels, exchange_and_iterate(): pl.pallas_call(functools.partial(kernel, nq, ne), out_shape=(jax.ShapeDty...  88.7 us
    unnamed x11, local copies, waits for them, and re-layouts  3.61 us

profile of v5, /device:TPU:1, one launch (start us, length us, event | category | flops | bytes accessed | tf_op | source)
XLA Modules:
  0.0 98.1 jit_solution(17660873239458543299)
XLA Ops:
  0.6 0.0 copy-start.1
  0.7 0.6 cosine_multiply_fusion
  1.3 0.4 copy-done.1
  1.6 0.2 copy.34
  1.8 0.3 fusion
  2.1 0.2 copy.35
  2.3 0.1 reshape.232.spec_ref
  2.4 0.1 copy.36
  2.5 0.0 copy-start.3
  2.5 0.6 copy-done.3
  3.2 0.2 convolution_convert_fusion.2
  3.5 0.3 convolution_convert_fusion
  3.8 0.0 copy-start.2
  3.8 0.1 reshape.234.own_ref
  3.9 0.6 copy-done.2
  4.5 0.1 stack.19
  4.6 0.1 stack.20
  4.7 0.1 copy.39
  4.7 0.1 copy.38
  4.8 0.1 copy.37
  4.9 0.0 copy-start
  4.9 0.1 reshape.235.triad_ref
  5.0 0.6 copy-done
  5.6 88.7 %shard_map.67 = (f32[8,1,128]{2,1,0:T(1,128)S(1)}, bf16[64,4,768]{2,1,0:T(4,128)(2,1)S(1)}, f32[2,256]{1,0:T(2,128)S(1)}) custom-call(bf16[64,3,4,256]{3,2,1,0:T(4,128)(2,1)S(1)} %reshape.232.spec_ref, bf16[64,4,768]{2,1,0:T(4,128)(2,1)S(1)} %reshape.234.own_ref, f32[256]{0:T(256)S(1)} %copy-done, s32[3,512]{1,0:T(4,128)S(1)} %reshape.235.triad_ref), custom_call_target="tpu_custom_call" | custom-call | tf_op jit(solution)/shard_map/pallas_call | solution.py:266
  94.3 0.5 broadcast.150
  94.8 0.7 reduce.11
  95.5 0.1 reshape.236
  95.7 0.7 reshape.237
  96.5 0.1 reshape.240
  96.6 0.2 convolution_bitcast_fusion
  96.9 0.7 copy.45
  97.6 0.6 copy.50
  (16 shorter events, 0.4 us)
Async XLA Ops:
  0.6 1.0 %copy-start.1 = (bf16[1,256,3,256]{3,1,2,0:T(8,128)(2,1)S(1)}, bf16[1,256,3,256]{3,1,2,0:T(8,128)(2,1)}, u32[]{:S(2)}) copy-start(bf16[1,256,3,256]{3,1,2,0:T(8,128)(2,1)} %param.4) | copy-start | bytes 1179652
  2.5 0.7 copy-start.3
  3.8 0.7 copy-start.2
  4.9 0.7 copy-start

commit v6 on v5

--- a/solution.py
+++ b/solution.py
@@ -32,10 +32,10 @@
 
 def kernel(
     nq, ne, spec_ref, own_ref, weight_ref, triad_ref,
-    last_ref, sums_ref, power_ref,
-    weight_rows, spec_all, flat, rows, prod_re, prod_im, sum_re, sum_im, field,
+    out_ref, sums_ref, power_ref,
+    last_ref, weight_rows, spec_all, flat, rows, prod_re, prod_im, sum_re, sum_im, field,
     coef_ref, part, part_in, piece, piece_in, mine, gathered, spread,
-    near_sem, send_sem, recv_sem,
+    send_sem, recv_sem,
 ):
     q = lax.axis_index("freq")
     e = lax.axis_index("space")
@@ -66,26 +66,15 @@
 
         lax.fori_loop(0, count - 1, step, 0)
 
-    def row(far_y, far_z):
-        rows_y = nq // ring
-        return {"freq": (q // ring + far_y) % rows_y * ring + (q % ring + far_z) % ring}
-
     def greet(device, _):
         pl.semaphore_signal(barrier, inc=1, device_id=device, device_id_type=MESH)
 
+    others("freq", nq, q, greet)
     others("space", ne, e, greet)
-    for far_y in range(1, nq // ring):
-        greet(row(far_y, 0), None)
-    for far_z in (1, ring - 1):
-        greet(row(0, far_z), None)
     for j in range(cols):
         value = weight_ref[(q * cols + j) % weight_ref.shape[0]]
         weight_rows[j * blocks : (j + 1) * blocks, :] = jnp.full((blocks, LANES), value)
-    pl.semaphore_wait(barrier, ne - 1 + nq // ring - 1 + 2)
-    for k, far_z in enumerate((1, 1, 2, 4)):
-        for other in (far_z, ring - far_z):
-            pl.semaphore_signal(near_sem.at[k], inc=1, device_id=row(0, other), device_id_type=MESH)
-        pl.semaphore_wait(near_sem.at[k], 2)
+    pl.semaphore_wait(barrier, nq + ne - 2)
 
     def exchange(slot, axis, count, index, source, target):
         def act(device, i):
@@ -229,8 +218,19 @@
                 precision=lax.Precision.HIGHEST, preferred_element_type=jnp.float32,
             )
             values = values * lax.rsqrt(energy / blocks + 1e-05)
-            for i in range(ne):
-                last_ref[i] = values[i : i + 1]
+            lane = lax.broadcasted_iota(jnp.int32, (2 * triads // nq, LANES), 1)
+            row_of = (2 * (lane // share % groups) + lane // nq) * 2 + lane // per_e % 2
+            own_row = row_of == lax.broadcasted_iota(jnp.int32, row_of.shape, 0)
+            wide = jnp.concatenate(
+                [jnp.where(own_row, values[i : i + 1], 0.0) for i in range(ne)], axis=1
+            )
+            k = lax.broadcasted_iota(jnp.int32, (ne * LANES, LANES), 0)
+            to = k // LANES * per_e + k % per_e
+            there = jnp.where(to == lax.broadcasted_iota(jnp.int32, to.shape, 1), 1.0, 0.0)
+            placed = jnp.dot(
+                wide, there, precision=lax.Precision.HIGHEST, preferred_element_type=jnp.float32
+            )
+            out_ref[...] = placed[:, :blocks]
             break
         got_mine = exchange(base + 5, "freq", nq, q, lambda i: mine.at[sweep], gathered)
         got_sums = exchange(1, "freq", nq, q, lambda i: own_ref.at[i], sums_ref)
@@ -266,13 +266,14 @@
     return pl.pallas_call(
         functools.partial(kernel, nq, ne),
         out_shape=(
-            jax.ShapeDtypeStruct((ne, 1, LANES), f32),
+            jax.ShapeDtypeStruct((2 * triads // nq, blocks), f32),
             jax.ShapeDtypeStruct(own.shape, bf16),
             jax.ShapeDtypeStruct((own.shape[1] // 2, own.shape[2] // 3), f32),
         ),
         in_specs=[vmem, vmem, pl.BlockSpec(memory_space=pltpu.SMEM), vmem],
         out_specs=(vmem, vmem, vmem),
         scratch_shapes=[
+            pltpu.VMEM((ne, 1, LANES), f32),
             pltpu.VMEM((cols * blocks, LANES), f32),
             pltpu.VMEM((blocks, bands, band, width), bf16),
             pltpu.VMEM((width // LANES, blocks * 16, LANES), f32),
@@ -290,7 +291,6 @@
             pltpu.VMEM((2, 1, LANES), f32),
             pltpu.VMEM((nq, 1, LANES), f32),
             pltpu.VMEM((ne, nq, 1, LANES), f32),
-            pltpu.SemaphoreType.REGULAR((4,)),
             pltpu.SemaphoreType.DMA((16,)),
             pltpu.SemaphoreType.DMA((16,)),
         ],
@@ -327,10 +327,9 @@
     first, second = triad_list[:, 0], triad_list[:, 1]
     triad = jnp.stack([first, second, first + second])
     triad = triad.reshape(3, nq, triads_here).transpose(0, 2, 1).reshape(3, triad_count)
-    last, sums, power_map = exchange_and_iterate(
+    vec, sums, power_map = exchange_and_iterate(
         nq, ne, spec.reshape(nq, cols // 4, 4, 2 * frequencies), own.reshape(nq, 2 * slots, columns), point_weights, triad
     )
-    vec = last.reshape(ne, 2, triads_here // 2, 2, nq // ne).transpose(2, 1, 3, 0, 4)
     coefficients = vec.reshape(triads_here, 2, nq)
     sums = sums.reshape(nq, slots, 2, columns)
     rounded = coefficients.astype(jnp.bfloat16).reshape(per_slot, slots, 2, nq)

time: 98.4 us -> 94.5 us (0.960)
  Pallas kernels: 88.7 us -> 86.4 us
    pallas_call x1, Pallas kernels: 88.7 us -> 86.4 us  [exchange_and_iterate(): pl.pallas_call(functools.partial(kernel, nq, ne), out_shape=(jax.ShapeDty...]
    unnamed x11 -> x12, local copies, waits for them, and re-layouts: 3.61 us -> 4.21 us
where the time goes in v6:
time: 94.5 us; the launch traced here: 94.3 us
  Pallas kernels  86.4 us (91%)
  local copies, waits for them, and re-layouts  5.33 us (6%)
  matrix products  0.98 us (1%)
    pallas_call x1, Pallas kernels, exchange_and_iterate(): pl.pallas_call(functools.partial(kernel, nq, ne), out_shape=(jax.ShapeDty...  86.4 us
    unnamed x12, local copies, waits for them, and re-layouts  4.21 us

profile of v6, /device:TPU:1, one launch (start us, length us, event | category | flops | bytes accessed | tf_op | source)
XLA Modules:
  0.0 94.3 jit_solution(9866478531846910464)
XLA Ops:
  0.6 0.0 copy-start.1
  0.7 0.6 cosine_multiply_fusion
  1.3 0.4 copy-done.1
  1.6 0.2 copy.31
  1.8 0.3 fusion
  2.1 0.2 copy.32
  2.3 0.1 reshape.229.spec_ref
  2.4 0.1 copy.33
  2.5 0.0 copy-start.3
  2.5 0.6 copy-done.3
  3.2 0.2 convolution_convert_fusion.2
  3.5 0.3 convolution_convert_fusion
  3.8 0.0 copy-start.2
  3.8 0.1 reshape.231.own_ref
  3.9 0.6 copy-done.2
  4.5 0.1 stack.19
  4.6 0.1 stack.20
  4.7 0.1 copy.36
  4.7 0.1 copy.35
  4.8 0.1 copy.34
  4.9 0.0 copy-start
  4.9 0.1 reshape.232.triad_ref
  5.0 0.6 copy-done
  5.6 86.4 %shard_map.67 = (f32[16,64]{1,0:T(8,128)S(1)}, bf16[64,4,768]{2,1,0:T(4,128)(2,1)S(1)}, f32[2,256]{1,0:T(2,128)S(1)}) custom-call(bf16[64,3,4,256]{3,2,1,0:T(4,128)(2,1)S(1)} %reshape.229.spec_ref, bf16[64,4,768]{2,1,0:T(4,128)(2,1)S(1)} %reshape.231.own_ref, f32[256]{0:T(256)S(1)} %copy-done, s32[3,512]{1,0:T(4,128)S(1)} %reshape.232.triad_ref), custom_call_target="tpu_custom_call" | custom-call | tf_op jit(solution)/shard_map/pallas_call | solution.py:266
  92.1 0.2 convolution_bitcast_fusion
  92.4 0.7 copy.41
  93.1 0.6 copy.51
  93.7 0.6 copy.52
  (14 shorter events, 0.3 us)
Async XLA Ops:
  0.6 1.0 %copy-start.1 = (bf16[1,256,3,256]{3,1,2,0:T(8,128)(2,1)S(1)}, bf16[1,256,3,256]{3,1,2,0:T(8,128)(2,1)}, u32[]{:S(2)}) copy-start(bf16[1,256,3,256]{3,1,2,0:T(8,128)(2,1)} %param.4) | copy-start | bytes 1179652
  2.5 0.7 copy-start.3
  3.8 0.7 copy-start.2
  4.9 0.7 copy-start

commit v7 on v6

--- a/solution.py
+++ b/solution.py
@@ -233,9 +233,10 @@
             out_ref[...] = placed[:, :blocks]
             break
         got_mine = exchange(base + 5, "freq", nq, q, lambda i: mine.at[sweep], gathered)
+        got_mine()
+        got_spread = exchange(base + 6, "space", ne, e, lambda i: gathered, spread)
         got_sums = exchange(1, "freq", nq, q, lambda i: own_ref.at[i], sums_ref)
-        got_mine()
-        exchange(base + 6, "space", ne, e, lambda i: gathered, spread)()
+        got_spread()
 
         def place(d, carry):
             for r in range(2):

time: 94.5 us -> 98.5 us (1.042)
  Pallas kernels: 86.4 us -> 90.5 us
    pallas_call x1, Pallas kernels: 86.4 us -> 90.5 us  [exchange_and_iterate(): pl.pallas_call(functools.partial(kernel, nq, ne), out_shape=(jax.ShapeDty...]
where the time goes in v7:
time: 98.5 us; the launch traced here: 98.3 us
  Pallas kernels  90.5 us (92%)
  local copies, waits for them, and re-layouts  5.33 us (5%)
    pallas_call x1, Pallas kernels, exchange_and_iterate(): pl.pallas_call(functools.partial(kernel, nq, ne), out_shape=(jax.ShapeDty...  90.5 us
    unnamed x12, local copies, waits for them, and re-layouts  4.21 us

profile of v7, /device:TPU:1, one launch (start us, length us, event | category | flops | bytes accessed | tf_op | source)
XLA Modules:
  0.0 98.3 jit_solution(5352708818764778292)
XLA Ops:
  0.6 0.0 copy-start.1
  0.7 0.6 cosine_multiply_fusion
  1.3 0.4 copy-done.1
  1.6 0.2 copy.31
  1.8 0.3 fusion
  2.1 0.2 copy.32
  2.3 0.1 reshape.229.spec_ref
  2.4 0.1 copy.33
  2.5 0.0 copy-start.3
  2.5 0.6 copy-done.3
  3.2 0.2 convolution_convert_fusion.2
  3.5 0.3 convolution_convert_fusion
  3.8 0.0 copy-start.2
  3.8 0.1 reshape.231.own_ref
  3.9 0.6 copy-done.2
  4.5 0.1 stack.19
  4.6 0.1 stack.20
  4.7 0.1 copy.36
  4.7 0.1 copy.35
  4.8 0.1 copy.34
  4.9 0.0 copy-start
  4.9 0.1 reshape.232.triad_ref
  5.0 0.6 copy-done
  5.6 90.5 %shard_map.67 = (f32[16,64]{1,0:T(8,128)S(1)}, bf16[64,4,768]{2,1,0:T(4,128)(2,1)S(1)}, f32[2,256]{1,0:T(2,128)S(1)}) custom-call(bf16[64,3,4,256]{3,2,1,0:T(4,128)(2,1)S(1)} %reshape.229.spec_ref, bf16[64,4,768]{2,1,0:T(4,128)(2,1)S(1)} %reshape.231.own_ref, f32[256]{0:T(256)S(1)} %copy-done, s32[3,512]{1,0:T(4,128)S(1)} %reshape.232.triad_ref), custom_call_target="tpu_custom_call" | custom-call | tf_op jit(solution)/shard_map/pallas_call | solution.py:267
  96.2 0.2 convolution_bitcast_fusion
  96.5 0.7 copy.41
  97.2 0.6 copy.51
  97.7 0.6 copy.52
  (14 shorter events, 0.3 us)
Async XLA Ops:
  0.6 1.0 %copy-start.1 = (bf16[1,256,3,256]{3,1,2,0:T(8,128)(2,1)S(1)}, bf16[1,256,3,256]{3,1,2,0:T(8,128)(2,1)}, u32[]{:S(2)}) copy-start(bf16[1,256,3,256]{3,1,2,0:T(8,128)(2,1)} %param.4) | copy-start | bytes 1179652
  2.5 0.7 copy-start.3
  3.8 0.7 copy-start.2
  4.9 0.7 copy-start
